TPU v7x, 128 devices: a whole 4x4x4 slice. The times are simulated.
128 devices in a mesh: gx: 8 (over y, core), gy: 16 (over z, x).
Axes of the slice: x: 4, y: 4, z: 4, core: 2. Of those that a mesh axis runs over, the one named last changes fastest.
Arguments:
- right_side: float32 [256, 512, 256], P('gx', 'gy'), may hold values from -32 to 32
- phase: int32 [256, 512, 256], P('gx', 'gy'), may hold values from 1 to 3
- table: float32 [4], replicated, may hold values from 0.3 to 3
Outputs:
- solution_field: float32 [256, 512, 256], P('gx', 'gy')
- residual: float32 [256, 512, 256], P('gx', 'gy')
- pre_residual: float32 [256, 512, 256], P('gx', 'gy')
- residual_image: float32 [256, 512, 256], P('gx', 'gy')
Inputs may be any that keep to these rules, and one draw needn't show every extreme that they name: `phase`: labels 1 slag, 2 steel, 3 argon plume; label 0 stands for the lining outside the grid.
All inputs are finite; a program needn't handle non-finite values.
Results may differ from a plain program's by a relative error of at most 0.0003.
Values sent between devices are 32-bit elements; how exact they have to be, the bound alone decides.
No kernel may reach another device: no remote copies, remote signals or barrier semaphores. Data moves between devices by JAX's collectives and lax.ppermute only.
A program may use at most 64 MiB of HBM per device.

v0:
```python
import jax
import jax.numpy as jnp
from jax import lax
from jax.sharding import PartitionSpec as P

ITERS = 2
centre_value = 1.1
half_width = 0.9
ratio_sigma = centre_value / half_width
rho_first = 1.0 / ratio_sigma
rho_second = 1.0 / (2.0 * ratio_sigma - rho_first)
rho_third = 1.0 / (2.0 * ratio_sigma - rho_second)
start_scale = 1.0 / centre_value
keep_first = rho_second * rho_first
push_first = 2.0 * rho_second / half_width
keep_second = rho_third * rho_second
push_second = 2.0 * rho_third / half_width


def extended(block, sides, width):
    for axis, dim in sides:
        count = lax.axis_size(axis)
        forward = [(i, i + 1) for i in range(count - 1)]
        backward = [(target, source) for source, target in forward]
        low = lax.ppermute(
            lax.slice_in_dim(block, block.shape[dim] - width, None, axis=dim), axis, forward
        )
        high = lax.ppermute(lax.slice_in_dim(block, 0, width, axis=dim), axis, backward)
        block = jnp.concatenate([low, block, high], axis=dim)
    return block


def harmonic(left, right):
    return 2.0 * left * right / (left + right)


def coupling_set(sigma_padded):
    centre = sigma_padded[1:-1, 1:-1, 1:-1]
    to_west = harmonic(centre, sigma_padded[:-2, 1:-1, 1:-1])
    to_east = harmonic(centre, sigma_padded[2:, 1:-1, 1:-1])
    to_south = harmonic(centre, sigma_padded[1:-1, :-2, 1:-1])
    to_north = harmonic(centre, sigma_padded[1:-1, 2:, 1:-1])
    to_down = harmonic(centre, sigma_padded[1:-1, 1:-1, :-2])
    to_up = harmonic(centre, sigma_padded[1:-1, 1:-1, 2:])
    diagonal = to_west + to_east + to_south + to_north + to_down + to_up
    return (to_west, to_east, to_south, to_north, to_down, to_up, diagonal)


def lookup(labels, table):
    return jnp.where(
        labels == 1,
        table[1],
        jnp.where(labels == 2, table[2], jnp.where(labels == 3, table[3], table[0])),
    )


def operate_ext(padded_xy, couplings):
    to_west, to_east, to_south, to_north, to_down, to_up, diagonal = couplings
    padded_z = jnp.pad(padded_xy, ((0, 0), (0, 0), (1, 1)))
    centre = padded_xy[1:-1, 1:-1]
    beside = (
        to_west * padded_xy[:-2, 1:-1]
        + to_east * padded_xy[2:, 1:-1]
        + to_south * padded_xy[1:-1, :-2]
        + to_north * padded_xy[1:-1, 2:]
        + to_down * padded_z[1:-1, 1:-1, :-2]
        + to_up * padded_z[1:-1, 1:-1, 2:]
    )
    return diagonal * centre - beside


def local(right_side, phase, table):
    labels_ext = extended(phase, (("gx", 0), ("gy", 1)), 1)
    sigma_ext = lookup(jnp.pad(labels_ext, ((0, 0), (0, 0), (1, 1))), table)
    stored_set = coupling_set(sigma_ext)

    def composite(vector):
        set_zero = tuple((member for member in stored_set))
        diagonal = set_zero[6]

        def image_of(field):
            return operate_ext(extended(field, (("gx", 0), ("gy", 1)), 1), set_zero)

        first = start_scale * (vector / diagonal)
        change = keep_first * first + push_first * ((vector - image_of(first)) / diagonal)
        second = first + change
        change = keep_second * change + push_second * ((vector - image_of(second)) / diagonal)
        third = second + change
        return (third, image_of(third))

    solution_field = jnp.zeros_like(right_side)
    residual = right_side
    pre_residual, residual_image = composite(residual)
    image_dir = jnp.zeros_like(right_side)
    pre_dir = jnp.zeros_like(right_side)
    resid_dir = jnp.zeros_like(right_side)
    direction = jnp.zeros_like(right_side)
    energy_prev = jnp.float32(1.0)
    step_prev = jnp.float32(1.0)
    for iteration in range(ITERS):
        energy_now, curvature = lax.psum(
            (jnp.sum(residual * pre_residual), jnp.sum(residual_image * pre_residual)), ("gx", "gy")
        )
        pre_image, double_image = composite(residual_image)
        if iteration == 0:
            step_size = energy_now / curvature
            image_dir = double_image
            pre_dir = pre_image
            resid_dir = residual_image
            direction = pre_residual
        else:
            momentum = energy_now / energy_prev
            step_size = energy_now / (curvature - momentum * energy_now / step_prev)
            image_dir = double_image + momentum * image_dir
            pre_dir = pre_image + momentum * pre_dir
            resid_dir = residual_image + momentum * resid_dir
            direction = pre_residual + momentum * direction
        solution_field = solution_field + step_size * direction
        residual = residual - step_size * resid_dir
        pre_residual = pre_residual - step_size * pre_dir
        residual_image = residual_image - step_size * image_dir
        energy_prev = energy_now
        step_prev = step_size
    return (solution_field, residual, pre_residual, residual_image)


def solution(mesh):
    placed = (P("gx", "gy", None), P("gx", "gy", None), P())
    return jax.shard_map(
        local,
        mesh=mesh,
        in_specs=placed,
        out_specs=(
            P("gx", "gy", None),
            P("gx", "gy", None),
            P("gx", "gy", None),
            P("gx", "gy", None),
        ),
        check_vma=False,
    )
```

profile of v0, /device:TPU:39, one launch (start us, length us, event | category | flops | bytes accessed | tf_op | source)
XLA Modules:
  0.0 359.8 jit_solution(430377248482108931)
XLA Ops:
  1.4 3.8 %collective-permute-start = (s32[1,32,256]{2,1,0:T(8,128)S(1)}, s32[1,32,256]{2,1,0:T(8,128)S(1)}, u32[]{:S(2)}, u32[]{:S(2)}) collective-permute-start(s32[1,32,256]{2,1,0:T(8,128)S(1)} %get-tuple-element.70), channel_id=1, source_target_pairs={{0,16},{16,32},{32,48},{48,64},{64,80},{80,96},{96,112},{1,17},{17... | collective-permute-start | bytes 98312 | tf_op jit(solution)/shard_map/ppermute | solution.py:25
  10.5 3.5 collective-permute-start.2
  16.5 4.3 %collective-permute-done.3 = s32[34,1,256]{2,1,0:T(1,128)S(1)} collective-permute-done((s32[34,1,256]{2,1,0:T(1,128)S(1)}, s32[34,1,256]{2,1,0:T(1,128)S(1)}, u32[]{:S(2)}, u32[]{:S(2)}) %collective-permute-start.3) | collective-permute-done | bytes 34848 | tf_op jit(solution)/shard_map/ppermute | solution.py:28
  26.5 3.3 collective-permute-start.4
  31.8 3.3 collective-permute-done.5
  37.1 3.4 collective-permute-start.7
  40.5 3.4 collective-permute-done.7
  57.8 3.4 collective-permute-start.11
  61.2 3.4 collective-permute-done.11
  78.6 3.4 collective-permute-start.15
  82.0 3.4 collective-permute-done.15
  86.4 3.3 multiply_reduce_fusion.2
  95.5 3.3 collective-permute-done.17
  100.8 3.5 collective-permute-start.19
  116.2 3.3 collective-permute-done.21
  121.5 3.4 collective-permute-start.23
  124.9 3.4 collective-permute-done.23
  137.0 3.3 collective-permute-done.25
  142.3 3.4 collective-permute-start.27
  145.7 63.7 %all-reduce.11 = (f32[]{:T(128)}, f32[]{:T(128)}) all-reduce(f32[]{:T(128)} %get-tuple-element.7, f32[]{:T(128)} %get-tuple-element.6), channel_id=1, replica_groups=mesh['gx'=8,'gy'=16] {'gx','gy'}, use_global_device_ids=true, to_apply=%region_1.2 | all-reduce | flops 2 | bytes 16 | tf_op jit(solution)/shard_map/psum | solution.py:101
  213.0 6.4 %fusion.125 = (f32[32,32,256]{2,1,0:T(8,128)S(1)}, f32[32,32,256]{2,1,0:T(8,128)S(1)}, f32[32,32,256]{2,1,0:T(8,128)}) fusion(f32[32,32,256]{2,1,0:T(8,128)S(1)} %copy-done.7, f32[32,32,256]{2,1,0:T(8,128)S(1)} %copy-done.4, f32[32,32,256]{2,1,0:T(8,128)S(1)} %copy-done.1, f32[32,32,256]{2,1,0:T(8,128)S(1)} %get-tuple-element.27, ...), kind=kLoop, calls=%fused_computation.275 | loop fusion | flops 7864320 | bytes 13766660 | tf_op jit(solution)/shard_map/mul | solution.py:84
  219.5 4.5 %collective-permute-start.28 = (f32[1,32,256]{2,1,0:T(8,128)S(1)}, f32[1,32,256]{2,1,0:T(8,128)S(1)}, u32[]{:S(2)}, u32[]{:S(2)}) collective-permute-start(f32[1,32,256]{2,1,0:T(8,128)S(1)} %get-tuple-element.55), channel_id=1, source_target_pairs={{0,16},{16,32},{32,48},{48,64},{64,80},{80,96},{96,112},{1,17},{17... | collective-permute-start | bytes 98312 | tf_op jit(solution)/shard_map/ppermute | solution.py:25
  229.3 3.3 collective-permute-start.30
  234.6 4.8 %collective-permute-done.31 = f32[34,1,256]{2,1,0:T(1,128)S(1)} collective-permute-done((f32[34,1,256]{2,1,0:T(1,128)S(1)}, f32[34,1,256]{2,1,0:T(1,128)S(1)}, u32[]{:S(2)}, u32[]{:S(2)}) %collective-permute-start.31) | collective-permute-done | bytes 34848 | tf_op jit(solution)/shard_map/ppermute | solution.py:28
  240.4 3.5 fusion.128
  243.9 3.3 collective-permute-start.32
  254.5 3.6 collective-permute-start.35
  259.3 62.3 %all-reduce.10 = (f32[]{:T(128)}, f32[]{:T(128)}) all-reduce(f32[]{:T(128)} %get-tuple-element.5, f32[]{:T(128)} %get-tuple-element.4), channel_id=1, replica_groups=mesh['gx'=8,'gy'=16] {'gx','gy'}, use_global_device_ids=true, to_apply=%region_5.6 | all-reduce | flops 2 | bytes 16 | tf_op jit(solution)/shard_map/psum | solution.py:101
  328.5 7.3 %multiply_subtract_fusion = (f32[32,32,256]{2,1,0:T(8,128)}, f32[32,32,256]{2,1,0:T(8,128)S(1)}) fusion(f32[32,32,256]{2,1,0:T(8,128)} %copy-done.9, f32[]{:T(128)S(6)} %div.70, f32[]{:T(128)S(6)} %div.72, f32[32,32,256]{2,1,0:T(8,128)} %copy-done.12, f32[]{:T(128)S(6)} %div.66, f32[32,32,256]{2,1,0:T(8,128)} %copy-done.23, f32[32,32,256]{2,1,0:T(8,128)} %copy-done.18, ...), kind=kLoop, calls=%fused_computation.254 | loop fusion | flops 9961472 | bytes 15863820 | tf_op jit(solution)/shard_map/sub | solution.py:120
  335.7 4.2 %collective-permute-start.36 = (f32[1,32,256]{2,1,0:T(8,128)S(1)}, f32[1,32,256]{2,1,0:T(8,128)S(1)}, u32[]{:S(2)}, u32[]{:S(2)}) collective-permute-start(f32[1,32,256]{2,1,0:T(8,128)S(1)} %get-tuple-element.51), channel_id=1, source_target_pairs={{0,16},{16,32},{32,48},{48,64},{64,80},{80,96},{96,112},{1,17},{17... | collective-permute-start | bytes 98312 | tf_op jit(solution)/shard_map/ppermute | solution.py:25
  345.2 3.3 collective-permute-start.38
  356.3 3.5 fusion.5
  (150 shorter events, 113.3 us)
Async XLA Ops:
  1.4 5.7 %collective-permute-start = (s32[1,32,256]{2,1,0:T(8,128)S(1)}, s32[1,32,256]{2,1,0:T(8,128)S(1)}, u32[]{:S(2)}, u32[]{:S(2)}) collective-permute-start(s32[1,32,256]{2,1,0:T(8,128)S(1)} %get-tuple-element.70), channel_id=1, source_target_pairs={{0,16},{16,32},{32,48},{48,64},{64,80},{80,96},{96,112},{1,17},{17... | collective-permute-start | bytes 98312 | tf_op jit(solution)/shard_map/ppermute | solution.py:25
  5.2 5.2 %collective-permute-start.1 = (s32[1,32,256]{2,1,0:T(8,128)S(1)}, s32[1,32,256]{2,1,0:T(8,128)S(1)}, u32[]{:S(2)}, u32[]{:S(2)}) collective-permute-start(s32[1,32,256]{2,1,0:T(8,128)S(1)} %get-tuple-element.69), channel_id=1, source_target_pairs={{16,0},{32,16},{48,32},{64,48},{80,64},{96,80},{112,96},{17,1},{33... | collective-permute-start | bytes 98312 | tf_op jit(solution)/shard_map/ppermute | solution.py:28
  10.5 6.0 %collective-permute-start.2 = (s32[34,1,256]{2,1,0:T(1,128)S(1)}, s32[34,1,256]{2,1,0:T(1,128)S(1)}, u32[]{:S(2)}, u32[]{:S(2)}) collective-permute-start(s32[34,1,256]{2,1,0:T(1,128)S(1)} %get-tuple-element.49), channel_id=1, source_target_pairs={{0,1},{1,2},{2,3},{3,4},{4,5},{5,6},{6,7},{7,8},{8,9},{9,10},{10,1... | collective-permute-start | bytes 104456 | tf_op jit(solution)/shard_map/ppermute | solution.py:25
  13.9 6.8 %collective-permute-start.3 = (s32[34,1,256]{2,1,0:T(1,128)S(1)}, s32[34,1,256]{2,1,0:T(1,128)S(1)}, u32[]{:S(2)}, u32[]{:S(2)}) collective-permute-start(s32[34,1,256]{2,1,0:T(1,128)S(1)} %get-tuple-element.50), channel_id=1, source_target_pairs={{1,0},{2,1},{3,2},{4,3},{5,4},{6,5},{7,6},{8,7},{9,8},{10,9},{11,1... | collective-permute-start | bytes 104456 | tf_op jit(solution)/shard_map/ppermute | solution.py:28
  26.5 5.3 %collective-permute-start.4 = (f32[1,32,256]{2,1,0:T(8,128)S(1)}, f32[1,32,256]{2,1,0:T(8,128)S(1)}, u32[]{:S(2)}, u32[]{:S(2)}) collective-permute-start(f32[1,32,256]{2,1,0:T(8,128)S(1)} %get-tuple-element.67), channel_id=1, source_target_pairs={{0,16},{16,32},{32,48},{48,64},{64,80},{80,96},{96,112},{1,17},{17... | collective-permute-start | bytes 98312 | tf_op jit(solution)/shard_map/ppermute | solution.py:25
  29.9 5.2 %collective-permute-start.5 = (f32[1,32,256]{2,1,0:T(8,128)S(1)}, f32[1,32,256]{2,1,0:T(8,128)S(1)}, u32[]{:S(2)}, u32[]{:S(2)}) collective-permute-start(f32[1,32,256]{2,1,0:T(8,128)S(1)} %get-tuple-element.68), channel_id=1, source_target_pairs={{16,0},{32,16},{48,32},{64,48},{80,64},{96,80},{112,96},{17,1},{33... | collective-permute-start | bytes 98312 | tf_op jit(solution)/shard_map/ppermute | solution.py:28
  35.2 5.3 %collective-permute-start.6 = (f32[34,1,256]{2,1,0:T(1,128)S(1)}, f32[34,1,256]{2,1,0:T(1,128)S(1)}, u32[]{:S(2)}, u32[]{:S(2)}) collective-permute-start(f32[34,1,256]{2,1,0:T(1,128)S(1)} %get-tuple-element.47), channel_id=1, source_target_pairs={{0,1},{1,2},{2,3},{3,4},{4,5},{5,6},{6,7},{7,8},{8,9},{9,10},{10,1... | collective-permute-start | bytes 104456 | tf_op jit(solution)/shard_map/ppermute | solution.py:25
  37.1 6.8 %collective-permute-start.7 = (f32[34,1,256]{2,1,0:T(1,128)S(1)}, f32[34,1,256]{2,1,0:T(1,128)S(1)}, u32[]{:S(2)}, u32[]{:S(2)}) collective-permute-start(f32[34,1,256]{2,1,0:T(1,128)S(1)} %get-tuple-element.48), channel_id=1, source_target_pairs={{1,0},{2,1},{3,2},{4,3},{5,4},{6,5},{7,6},{8,7},{9,8},{10,9},{11,1... | collective-permute-start | bytes 104456 | tf_op jit(solution)/shard_map/ppermute | solution.py:28
  50.6 5.2 %collective-permute-start.9 = (f32[1,32,256]{2,1,0:T(8,128)S(1)}, f32[1,32,256]{2,1,0:T(8,128)S(1)}, u32[]{:S(2)}, u32[]{:S(2)}) collective-permute-start(f32[1,32,256]{2,1,0:T(8,128)S(1)} %get-tuple-element.66), channel_id=1, source_target_pairs={{16,0},{32,16},{48,32},{64,48},{80,64},{96,80},{112,96},{17,1},{33... | collective-permute-start | bytes 98312 | tf_op jit(solution)/shard_map/ppermute | solution.py:28
  55.9 5.3 %collective-permute-start.10 = (f32[34,1,256]{2,1,0:T(1,128)S(1)}, f32[34,1,256]{2,1,0:T(1,128)S(1)}, u32[]{:S(2)}, u32[]{:S(2)}) collective-permute-start(f32[34,1,256]{2,1,0:T(1,128)S(1)} %get-tuple-element.45), channel_id=1, source_target_pairs={{0,1},{1,2},{2,3},{3,4},{4,5},{5,6},{6,7},{7,8},{8,9},{9,10},{10,1... | collective-permute-start | bytes 104456 | tf_op jit(solution)/shard_map/ppermute | solution.py:25
  57.8 6.8 %collective-permute-start.11 = (f32[34,1,256]{2,1,0:T(1,128)S(1)}, f32[34,1,256]{2,1,0:T(1,128)S(1)}, u32[]{:S(2)}, u32[]{:S(2)}) collective-permute-start(f32[34,1,256]{2,1,0:T(1,128)S(1)} %get-tuple-element.46), channel_id=1, source_target_pairs={{1,0},{2,1},{3,2},{4,3},{5,4},{6,5},{7,6},{8,7},{9,8},{10,9},{11,1... | collective-permute-start | bytes 104456 | tf_op jit(solution)/shard_map/ppermute | solution.py:28
  71.4 5.2 %collective-permute-start.13 = (f32[1,32,256]{2,1,0:T(8,128)S(1)}, f32[1,32,256]{2,1,0:T(8,128)S(1)}, u32[]{:S(2)}, u32[]{:S(2)}) collective-permute-start(f32[1,32,256]{2,1,0:T(8,128)S(1)} %get-tuple-element.64), channel_id=1, source_target_pairs={{16,0},{32,16},{48,32},{64,48},{80,64},{96,80},{112,96},{17,1},{33... | collective-permute-start | bytes 98312 | tf_op jit(solution)/shard_map/ppermute | solution.py:28
  76.7 5.3 %collective-permute-start.14 = (f32[34,1,256]{2,1,0:T(1,128)S(1)}, f32[34,1,256]{2,1,0:T(1,128)S(1)}, u32[]{:S(2)}, u32[]{:S(2)}) collective-permute-start(f32[34,1,256]{2,1,0:T(1,128)S(1)} %get-tuple-element.43), channel_id=1, source_target_pairs={{0,1},{1,2},{2,3},{3,4},{4,5},{5,6},{6,7},{7,8},{8,9},{9,10},{10,1... | collective-permute-start | bytes 104456 | tf_op jit(solution)/shard_map/ppermute | solution.py:25
  78.6 6.8 %collective-permute-start.15 = (f32[34,1,256]{2,1,0:T(1,128)S(1)}, f32[34,1,256]{2,1,0:T(1,128)S(1)}, u32[]{:S(2)}, u32[]{:S(2)}) collective-permute-start(f32[34,1,256]{2,1,0:T(1,128)S(1)} %get-tuple-element.44), channel_id=1, source_target_pairs={{1,0},{2,1},{3,2},{4,3},{5,4},{6,5},{7,6},{8,7},{9,8},{10,9},{11,1... | collective-permute-start | bytes 104456 | tf_op jit(solution)/shard_map/ppermute | solution.py:28
  93.6 5.2 %collective-permute-start.17 = (f32[1,32,256]{2,1,0:T(8,128)S(1)}, f32[1,32,256]{2,1,0:T(8,128)S(1)}, u32[]{:S(2)}, u32[]{:S(2)}) collective-permute-start(f32[1,32,256]{2,1,0:T(8,128)S(1)} %get-tuple-element.62), channel_id=1, source_target_pairs={{16,0},{32,16},{48,32},{64,48},{80,64},{96,80},{112,96},{17,1},{33... | collective-permute-start | bytes 98312 | tf_op jit(solution)/shard_map/ppermute | solution.py:28
  98.8 5.5 %collective-permute-start.18 = (f32[34,1,256]{2,1,0:T(1,128)S(1)}, f32[34,1,256]{2,1,0:T(1,128)S(1)}, u32[]{:S(2)}, u32[]{:S(2)}) collective-permute-start(f32[34,1,256]{2,1,0:T(1,128)S(1)} %get-tuple-element.41), channel_id=1, source_target_pairs={{0,1},{1,2},{2,3},{3,4},{4,5},{5,6},{6,7},{7,8},{8,9},{9,10},{10,1... | collective-permute-start | bytes 104456 | tf_op jit(solution)/shard_map/ppermute | solution.py:25
  100.8 6.8 %collective-permute-start.19 = (f32[34,1,256]{2,1,0:T(1,128)S(1)}, f32[34,1,256]{2,1,0:T(1,128)S(1)}, u32[]{:S(2)}, u32[]{:S(2)}) collective-permute-start(f32[34,1,256]{2,1,0:T(1,128)S(1)} %get-tuple-element.42), channel_id=1, source_target_pairs={{1,0},{2,1},{3,2},{4,3},{5,4},{6,5},{7,6},{8,7},{9,8},{10,9},{11,1... | collective-permute-start | bytes 104456 | tf_op jit(solution)/shard_map/ppermute | solution.py:28
  114.3 5.2 %collective-permute-start.21 = (f32[1,32,256]{2,1,0:T(8,128)S(1)}, f32[1,32,256]{2,1,0:T(8,128)S(1)}, u32[]{:S(2)}, u32[]{:S(2)}) collective-permute-start(f32[1,32,256]{2,1,0:T(8,128)S(1)} %get-tuple-element.60), channel_id=1, source_target_pairs={{16,0},{32,16},{48,32},{64,48},{80,64},{96,80},{112,96},{17,1},{33... | collective-permute-start | bytes 98312 | tf_op jit(solution)/shard_map/ppermute | solution.py:28
  119.6 5.3 %collective-permute-start.22 = (f32[34,1,256]{2,1,0:T(1,128)S(1)}, f32[34,1,256]{2,1,0:T(1,128)S(1)}, u32[]{:S(2)}, u32[]{:S(2)}) collective-permute-start(f32[34,1,256]{2,1,0:T(1,128)S(1)} %get-tuple-element.39), channel_id=1, source_target_pairs={{0,1},{1,2},{2,3},{3,4},{4,5},{5,6},{6,7},{7,8},{8,9},{9,10},{10,1... | collective-permute-start | bytes 104456 | tf_op jit(solution)/shard_map/ppermute | solution.py:25
  121.5 6.8 %collective-permute-start.23 = (f32[34,1,256]{2,1,0:T(1,128)S(1)}, f32[34,1,256]{2,1,0:T(1,128)S(1)}, u32[]{:S(2)}, u32[]{:S(2)}) collective-permute-start(f32[34,1,256]{2,1,0:T(1,128)S(1)} %get-tuple-element.40), channel_id=1, source_target_pairs={{1,0},{2,1},{3,2},{4,3},{5,4},{6,5},{7,6},{8,7},{9,8},{10,9},{11,1... | collective-permute-start | bytes 104456 | tf_op jit(solution)/shard_map/ppermute | solution.py:28
  140.4 70.3 %collective-permute-start.26 = (f32[34,1,256]{2,1,0:T(1,128)S(1)}, f32[34,1,256]{2,1,0:T(1,128)S(1)}, u32[]{:S(2)}, u32[]{:S(2)}) collective-permute-start(f32[34,1,256]{2,1,0:T(1,128)S(1)} %get-tuple-element.37), channel_id=1, source_target_pairs={{0,1},{1,2},{2,3},{3,4},{4,5},{5,6},{6,7},{7,8},{8,9},{9,10},{10,1... | collective-permute-start | bytes 104456 | tf_op jit(solution)/shard_map/ppermute | solution.py:25
  142.3 68.4 %collective-permute-start.27 = (f32[34,1,256]{2,1,0:T(1,128)S(1)}, f32[34,1,256]{2,1,0:T(1,128)S(1)}, u32[]{:S(2)}, u32[]{:S(2)}) collective-permute-start(f32[34,1,256]{2,1,0:T(1,128)S(1)} %get-tuple-element.38), channel_id=1, source_target_pairs={{1,0},{2,1},{3,2},{4,3},{5,4},{6,5},{7,6},{8,7},{9,8},{10,9},{11,1... | collective-permute-start | bytes 104456 | tf_op jit(solution)/shard_map/ppermute | solution.py:28
  219.5 6.4 %collective-permute-start.28 = (f32[1,32,256]{2,1,0:T(8,128)S(1)}, f32[1,32,256]{2,1,0:T(8,128)S(1)}, u32[]{:S(2)}, u32[]{:S(2)}) collective-permute-start(f32[1,32,256]{2,1,0:T(8,128)S(1)} %get-tuple-element.55), channel_id=1, source_target_pairs={{0,16},{16,32},{32,48},{48,64},{64,80},{80,96},{96,112},{1,17},{17... | collective-permute-start | bytes 98312 | tf_op jit(solution)/shard_map/ppermute | solution.py:25
  229.3 5.3 %collective-permute-start.30 = (f32[34,1,256]{2,1,0:T(1,128)S(1)}, f32[34,1,256]{2,1,0:T(1,128)S(1)}, u32[]{:S(2)}, u32[]{:S(2)}) collective-permute-start(f32[34,1,256]{2,1,0:T(1,128)S(1)} %get-tuple-element.35), channel_id=1, source_target_pairs={{0,1},{1,2},{2,3},{3,4},{4,5},{5,6},{6,7},{7,8},{8,9},{9,10},{10,1... | collective-permute-start | bytes 104456 | tf_op jit(solution)/shard_map/ppermute | solution.py:25
  232.6 6.8 %collective-permute-start.31 = (f32[34,1,256]{2,1,0:T(1,128)S(1)}, f32[34,1,256]{2,1,0:T(1,128)S(1)}, u32[]{:S(2)}, u32[]{:S(2)}) collective-permute-start(f32[34,1,256]{2,1,0:T(1,128)S(1)} %get-tuple-element.36), channel_id=1, source_target_pairs={{1,0},{2,1},{3,2},{4,3},{5,4},{6,5},{7,6},{8,7},{9,8},{10,9},{11,1... | collective-permute-start | bytes 104456 | tf_op jit(solution)/shard_map/ppermute | solution.py:28
  243.9 5.3 %collective-permute-start.32 = (f32[1,32,256]{2,1,0:T(8,128)S(1)}, f32[1,32,256]{2,1,0:T(8,128)S(1)}, u32[]{:S(2)}, u32[]{:S(2)}) collective-permute-start(f32[1,32,256]{2,1,0:T(8,128)S(1)} %get-tuple-element.53), channel_id=1, source_target_pairs={{0,16},{16,32},{32,48},{48,64},{64,80},{80,96},{96,112},{1,17},{17... | collective-permute-start | bytes 98312 | tf_op jit(solution)/shard_map/ppermute | solution.py:25
  252.6 73.5 %collective-permute-start.34 = (f32[34,1,256]{2,1,0:T(1,128)S(1)}, f32[34,1,256]{2,1,0:T(1,128)S(1)}, u32[]{:S(2)}, u32[]{:S(2)}) collective-permute-start(f32[34,1,256]{2,1,0:T(1,128)S(1)} %get-tuple-element.33), channel_id=1, source_target_pairs={{0,1},{1,2},{2,3},{3,4},{4,5},{5,6},{6,7},{7,8},{8,9},{9,10},{10,1... | collective-permute-start | bytes 104456 | tf_op jit(solution)/shard_map/ppermute | solution.py:25
  254.5 71.6 %collective-permute-start.35 = (f32[34,1,256]{2,1,0:T(1,128)S(1)}, f32[34,1,256]{2,1,0:T(1,128)S(1)}, u32[]{:S(2)}, u32[]{:S(2)}) collective-permute-start(f32[34,1,256]{2,1,0:T(1,128)S(1)} %get-tuple-element.34), channel_id=1, source_target_pairs={{1,0},{2,1},{3,2},{4,3},{5,4},{6,5},{7,6},{8,7},{9,8},{10,9},{11,1... | collective-permute-start | bytes 104456 | tf_op jit(solution)/shard_map/ppermute | solution.py:28
  335.7 6.1 %collective-permute-start.36 = (f32[1,32,256]{2,1,0:T(8,128)S(1)}, f32[1,32,256]{2,1,0:T(8,128)S(1)}, u32[]{:S(2)}, u32[]{:S(2)}) collective-permute-start(f32[1,32,256]{2,1,0:T(8,128)S(1)} %get-tuple-element.51), channel_id=1, source_target_pairs={{0,16},{16,32},{32,48},{48,64},{64,80},{80,96},{96,112},{1,17},{17... | collective-permute-start | bytes 98312 | tf_op jit(solution)/shard_map/ppermute | solution.py:25
  339.9 5.2 %collective-permute-start.37 = (f32[1,32,256]{2,1,0:T(8,128)S(1)}, f32[1,32,256]{2,1,0:T(8,128)S(1)}, u32[]{:S(2)}, u32[]{:S(2)}) collective-permute-start(f32[1,32,256]{2,1,0:T(8,128)S(1)} %get-tuple-element.52), channel_id=1, source_target_pairs={{16,0},{32,16},{48,32},{64,48},{80,64},{96,80},{112,96},{17,1},{33... | collective-permute-start | bytes 98312 | tf_op jit(solution)/shard_map/ppermute | solution.py:28
  345.2 7.3 %collective-permute-start.38 = (f32[34,1,256]{2,1,0:T(1,128)S(1)}, f32[34,1,256]{2,1,0:T(1,128)S(1)}, u32[]{:S(2)}, u32[]{:S(2)}) collective-permute-start(f32[34,1,256]{2,1,0:T(1,128)S(1)} %get-tuple-element.31), channel_id=1, source_target_pairs={{0,1},{1,2},{2,3},{3,4},{4,5},{5,6},{6,7},{7,8},{8,9},{9,10},{10,1... | collective-permute-start | bytes 104456 | tf_op jit(solution)/shard_map/ppermute | solution.py:25
  348.5 6.8 %collective-permute-start.39 = (f32[34,1,256]{2,1,0:T(1,128)S(1)}, f32[34,1,256]{2,1,0:T(1,128)S(1)}, u32[]{:S(2)}, u32[]{:S(2)}) collective-permute-start(f32[34,1,256]{2,1,0:T(1,128)S(1)} %get-tuple-element.32), channel_id=1, source_target_pairs={{1,0},{2,1},{3,2},{4,3},{5,4},{6,5},{7,6},{8,7},{9,8},{10,9},{11,1... | collective-permute-start | bytes 104456 | tf_op jit(solution)/shard_map/ppermute | solution.py:28
  (34 other events, 686.7 us)
where the time goes:
time: 361 us; the launch traced here: 360 us
  blocking collectives  126 us (35%)
  starting transfers between devices  107 us (30%)
  waiting for transfers between devices  60.4 us (17%)
  other arithmetic  56.1 us (16%)
  between operations  7.42 us (2%)
    psum x2, blocking collectives, local(): lax.psum((jnp.sum(residual * pre_residual), jnp.sum(residual_image * pre_...  126 us
    ppermute x20, waiting for transfers between devices, extended(): lax.ppermute(lax.slice_in_dim(block, 0, width, axis=dim), axis, backward)  60.4 us
    ppermute x20, starting transfers between devices, extended(): lax.ppermute(lax.slice_in_dim(block, block.shape[dim] - width, None, axis...  57.9 us
    ppermute x20, starting transfers between devices, extended(): lax.ppermute(lax.slice_in_dim(block, 0, width, axis=dim), axis, backward)  49 us
    concatenate x10, other arithmetic, extended(): block = jnp.concatenate([low, block, high], axis=dim)  11.3 us
    mul x3, other arithmetic, composite(): first = start_scale * (vector / diagonal)  9.5 us
    add x3, other arithmetic, composite(): second = first + change  8.92 us
    sub x1, other arithmetic, local(): pre_residual = pre_residual - step_size * pre_dir  7.26 us
  transfers between devices with their start and end apart: 40, of which 18 were waited for; matrix products, arithmetic and copies ran while one was open for 1% of the time, Pallas kernels for 0%

commit v1 on v0

--- a/solution.py
+++ b/solution.py
@@ -99,7 +99,10 @@
     step_prev = jnp.float32(1.0)
     for iteration in range(ITERS):
         energy_now, curvature = lax.psum(
-            (jnp.sum(residual * pre_residual), jnp.sum(residual_image * pre_residual)), ("gx", "gy")
+            lax.psum(
+                (jnp.sum(residual * pre_residual), jnp.sum(residual_image * pre_residual)), "gy"
+            ),
+            "gx",
         )
         pre_image, double_image = composite(residual_image)
         if iteration == 0:

time: 361 us -> 322 us (0.89)
  blocking collectives: 126 us -> 85.9 us
    psum x2, blocking collectives: 126 us -> 48.6 us  [local(): lax.psum((jnp.sum(residual * pre_residual), jnp.sum(residual_image * pre_...]
    psum x0 -> x2, blocking collectives: none -> 37.4 us  [local(): lax.psum(lax.psum((jnp.sum(residual * pre_residual), jnp.sum(residual_ima...]
  transfers between devices with their start and end apart: 40 -> 40, of which waited for: 18 -> 18; matrix products, arithmetic and copies ran while one was open for 1% -> 2% of each run, Pallas kernels for 0% -> 0%
where the time goes in v1:
time: 322 us; the launch traced here: 321 us
  starting transfers between devices  108 us (34%)
  blocking collectives  85.9 us (27%)
  waiting for transfers between devices  59.8 us (19%)
  other arithmetic  56.4 us (18%)
  between operations  7.72 us (2%)
    ppermute x20, waiting for transfers between devices, extended(): lax.ppermute(lax.slice_in_dim(block, 0, width, axis=dim), axis, backward)  59.8 us
    ppermute x20, starting transfers between devices, extended(): lax.ppermute(lax.slice_in_dim(block, block.shape[dim] - width, None, axis...  58.3 us
    ppermute x20, starting transfers between devices, extended(): lax.ppermute(lax.slice_in_dim(block, 0, width, axis=dim), axis, backward)  49.4 us
    psum x2, blocking collectives, local(): lax.psum((jnp.sum(residual * pre_residual), jnp.sum(residual_image * pre_...  48.6 us
    psum x2, blocking collectives, local(): lax.psum(lax.psum((jnp.sum(residual * pre_residual), jnp.sum(residual_ima...  37.4 us
    concatenate x10, other arithmetic, extended(): block = jnp.concatenate([low, block, high], axis=dim)  11.3 us
    mul x3, other arithmetic, composite(): first = start_scale * (vector / diagonal)  9.67 us
    add x3, other arithmetic, composite(): second = first + change  8.9 us
  transfers between devices with their start and end apart: 40, of which 18 were waited for; matrix products, arithmetic and copies ran while one was open for 2% of the time, Pallas kernels for 0%

profile of v1, /device:TPU:39, one launch (start us, length us, event | category | flops | bytes accessed | tf_op | source)
XLA Modules:
  0.0 320.5 jit_solution(18513038543344012)
XLA Ops:
  1.4 3.8 %collective-permute-start = (s32[1,32,256]{2,1,0:T(8,128)S(1)}, s32[1,32,256]{2,1,0:T(8,128)S(1)}, u32[]{:S(2)}, u32[]{:S(2)}) collective-permute-start(s32[1,32,256]{2,1,0:T(8,128)S(1)} %get-tuple-element.74), channel_id=1, source_target_pairs={{0,16},{16,32},{32,48},{48,64},{64,80},{80,96},{96,112},{1,17},{17... | collective-permute-start | bytes 98312 | tf_op jit(solution)/shard_map/ppermute | solution.py:25
  10.5 3.5 %collective-permute-start.2 = (s32[34,1,256]{2,1,0:T(1,128)S(1)}, s32[34,1,256]{2,1,0:T(1,128)S(1)}, u32[]{:S(2)}, u32[]{:S(2)}) collective-permute-start(s32[34,1,256]{2,1,0:T(1,128)S(1)} %get-tuple-element.53), channel_id=1, source_target_pairs={{0,1},{1,2},{2,3},{3,4},{4,5},{5,6},{6,7},{7,8},{8,9},{9,10},{10,1... | collective-permute-start | bytes 104456 | tf_op jit(solution)/shard_map/ppermute | solution.py:25
  16.5 4.3 %collective-permute-done.3 = s32[34,1,256]{2,1,0:T(1,128)S(1)} collective-permute-done((s32[34,1,256]{2,1,0:T(1,128)S(1)}, s32[34,1,256]{2,1,0:T(1,128)S(1)}, u32[]{:S(2)}, u32[]{:S(2)}) %collective-permute-start.3) | collective-permute-done | bytes 34848 | tf_op jit(solution)/shard_map/ppermute | solution.py:28
  26.5 3.3 %collective-permute-start.4 = (f32[1,32,256]{2,1,0:T(8,128)S(1)}, f32[1,32,256]{2,1,0:T(8,128)S(1)}, u32[]{:S(2)}, u32[]{:S(2)}) collective-permute-start(f32[1,32,256]{2,1,0:T(8,128)S(1)} %get-tuple-element.71), channel_id=1, source_target_pairs={{0,16},{16,32},{32,48},{48,64},{64,80},{80,96},{96,112},{1,17},{17... | collective-permute-start | bytes 98312 | tf_op jit(solution)/shard_map/ppermute | solution.py:25
  31.8 3.3 %collective-permute-done.5 = f32[1,32,256]{2,1,0:T(8,128)S(1)} collective-permute-done((f32[1,32,256]{2,1,0:T(8,128)S(1)}, f32[1,32,256]{2,1,0:T(8,128)S(1)}, u32[]{:S(2)}, u32[]{:S(2)}) %collective-permute-start.5) | collective-permute-done | bytes 32800 | tf_op jit(solution)/shard_map/ppermute | solution.py:28
  37.1 3.4 %collective-permute-start.7 = (f32[34,1,256]{2,1,0:T(1,128)S(1)}, f32[34,1,256]{2,1,0:T(1,128)S(1)}, u32[]{:S(2)}, u32[]{:S(2)}) collective-permute-start(f32[34,1,256]{2,1,0:T(1,128)S(1)} %get-tuple-element.52), channel_id=1, source_target_pairs={{1,0},{2,1},{3,2},{4,3},{5,4},{6,5},{7,6},{8,7},{9,8},{10,9},{11,1... | collective-permute-start | bytes 104456 | tf_op jit(solution)/shard_map/ppermute | solution.py:28
  40.5 3.4 %collective-permute-done.7 = f32[34,1,256]{2,1,0:T(1,128)S(1)} collective-permute-done((f32[34,1,256]{2,1,0:T(1,128)S(1)}, f32[34,1,256]{2,1,0:T(1,128)S(1)}, u32[]{:S(2)}, u32[]{:S(2)}) %collective-permute-start.7) | collective-permute-done | bytes 34848 | tf_op jit(solution)/shard_map/ppermute | solution.py:28
  57.8 3.4 %collective-permute-start.11 = (f32[34,1,256]{2,1,0:T(1,128)S(1)}, f32[34,1,256]{2,1,0:T(1,128)S(1)}, u32[]{:S(2)}, u32[]{:S(2)}) collective-permute-start(f32[34,1,256]{2,1,0:T(1,128)S(1)} %get-tuple-element.50), channel_id=1, source_target_pairs={{1,0},{2,1},{3,2},{4,3},{5,4},{6,5},{7,6},{8,7},{9,8},{10,9},{11,1... | collective-permute-start | bytes 104456 | tf_op jit(solution)/shard_map/ppermute | solution.py:28
  61.2 3.4 %collective-permute-done.11 = f32[34,1,256]{2,1,0:T(1,128)S(1)} collective-permute-done((f32[34,1,256]{2,1,0:T(1,128)S(1)}, f32[34,1,256]{2,1,0:T(1,128)S(1)}, u32[]{:S(2)}, u32[]{:S(2)}) %collective-permute-start.11) | collective-permute-done | bytes 34848 | tf_op jit(solution)/shard_map/ppermute | solution.py:28
  78.6 3.4 %collective-permute-start.15 = (f32[34,1,256]{2,1,0:T(1,128)S(1)}, f32[34,1,256]{2,1,0:T(1,128)S(1)}, u32[]{:S(2)}, u32[]{:S(2)}) collective-permute-start(f32[34,1,256]{2,1,0:T(1,128)S(1)} %get-tuple-element.48), channel_id=1, source_target_pairs={{1,0},{2,1},{3,2},{4,3},{5,4},{6,5},{7,6},{8,7},{9,8},{10,9},{11,1... | collective-permute-start | bytes 104456 | tf_op jit(solution)/shard_map/ppermute | solution.py:28
  82.0 3.4 %collective-permute-done.15 = f32[34,1,256]{2,1,0:T(1,128)S(1)} collective-permute-done((f32[34,1,256]{2,1,0:T(1,128)S(1)}, f32[34,1,256]{2,1,0:T(1,128)S(1)}, u32[]{:S(2)}, u32[]{:S(2)}) %collective-permute-start.15) | collective-permute-done | bytes 34848 | tf_op jit(solution)/shard_map/ppermute | solution.py:28
  95.5 3.3 %collective-permute-done.17 = f32[1,32,256]{2,1,0:T(8,128)S(1)} collective-permute-done((f32[1,32,256]{2,1,0:T(8,128)S(1)}, f32[1,32,256]{2,1,0:T(8,128)S(1)}, u32[]{:S(2)}, u32[]{:S(2)}) %collective-permute-start.17) | collective-permute-done | bytes 32800 | tf_op jit(solution)/shard_map/ppermute | solution.py:28
  100.7 3.5 %collective-permute-start.19 = (f32[34,1,256]{2,1,0:T(1,128)S(1)}, f32[34,1,256]{2,1,0:T(1,128)S(1)}, u32[]{:S(2)}, u32[]{:S(2)}) collective-permute-start(f32[34,1,256]{2,1,0:T(1,128)S(1)} %get-tuple-element.46), channel_id=1, source_target_pairs={{1,0},{2,1},{3,2},{4,3},{5,4},{6,5},{7,6},{8,7},{9,8},{10,9},{11,1... | collective-permute-start | bytes 104456 | tf_op jit(solution)/shard_map/ppermute | solution.py:28
  116.2 3.3 %collective-permute-done.21 = f32[1,32,256]{2,1,0:T(8,128)S(1)} collective-permute-done((f32[1,32,256]{2,1,0:T(8,128)S(1)}, f32[1,32,256]{2,1,0:T(8,128)S(1)}, u32[]{:S(2)}, u32[]{:S(2)}) %collective-permute-start.21) | collective-permute-done | bytes 32800 | tf_op jit(solution)/shard_map/ppermute | solution.py:28
  121.5 3.4 %collective-permute-start.23 = (f32[34,1,256]{2,1,0:T(1,128)S(1)}, f32[34,1,256]{2,1,0:T(1,128)S(1)}, u32[]{:S(2)}, u32[]{:S(2)}) collective-permute-start(f32[34,1,256]{2,1,0:T(1,128)S(1)} %get-tuple-element.44), channel_id=1, source_target_pairs={{1,0},{2,1},{3,2},{4,3},{5,4},{6,5},{7,6},{8,7},{9,8},{10,9},{11,1... | collective-permute-start | bytes 104456 | tf_op jit(solution)/shard_map/ppermute | solution.py:28
  124.8 3.4 %collective-permute-done.23 = f32[34,1,256]{2,1,0:T(1,128)S(1)} collective-permute-done((f32[34,1,256]{2,1,0:T(1,128)S(1)}, f32[34,1,256]{2,1,0:T(1,128)S(1)}, u32[]{:S(2)}, u32[]{:S(2)}) %collective-permute-start.23) | collective-permute-done | bytes 34848 | tf_op jit(solution)/shard_map/ppermute | solution.py:28
  137.0 3.3 %collective-permute-done.25 = f32[1,32,256]{2,1,0:T(8,128)S(1)} collective-permute-done((f32[1,32,256]{2,1,0:T(8,128)S(1)}, f32[1,32,256]{2,1,0:T(8,128)S(1)}, u32[]{:S(2)}, u32[]{:S(2)}) %collective-permute-start.25) | collective-permute-done | bytes 32800 | tf_op jit(solution)/shard_map/ppermute | solution.py:28
  142.3 3.4 %collective-permute-start.27 = (f32[34,1,256]{2,1,0:T(1,128)S(1)}, f32[34,1,256]{2,1,0:T(1,128)S(1)}, u32[]{:S(2)}, u32[]{:S(2)}) collective-permute-start(f32[34,1,256]{2,1,0:T(1,128)S(1)} %get-tuple-element.42), channel_id=1, source_target_pairs={{1,0},{2,1},{3,2},{4,3},{5,4},{6,5},{7,6},{8,7},{9,8},{10,9},{11,1... | collective-permute-start | bytes 104456 | tf_op jit(solution)/shard_map/ppermute | solution.py:28
  145.7 24.2 %all-reduce.11 = (f32[]{:T(128)}, f32[]{:T(128)}) all-reduce(f32[]{:T(128)} %get-tuple-element.7, f32[]{:T(128)} %get-tuple-element.6), channel_id=1, replica_groups=mesh['gx'=8,'gy'=16] {'gy'}, use_global_device_ids=true, to_apply=%region_1.2 | all-reduce | flops 2 | bytes 16 | tf_op jit(solution)/shard_map/psum | solution.py:102
  169.9 19.0 %all-reduce.13 = (f32[]{:T(128)}, f32[]{:T(128)}) all-reduce(f32[]{:T(128)} %get-tuple-element.10, f32[]{:T(128)} %get-tuple-element.11), channel_id=1, replica_groups=mesh['gx'=8,'gy'=16] {'gx'}, use_global_device_ids=true, to_apply=%region_2.3 | all-reduce | flops 2 | bytes 16 | tf_op jit(solution)/shard_map/psum | solution.py:101
  192.6 6.6 %fusion.125 = (f32[32,32,256]{2,1,0:T(8,128)S(1)}, f32[32,32,256]{2,1,0:T(8,128)S(1)}, f32[32,32,256]{2,1,0:T(8,128)}) fusion(f32[32,32,256]{2,1,0:T(8,128)S(1)} %copy-done.7, f32[32,32,256]{2,1,0:T(8,128)S(1)} %copy-done.4, f32[32,32,256]{2,1,0:T(8,128)S(1)} %copy-done.1, f32[32,32,256]{2,1,0:T(8,128)S(1)} %get-tuple-element.31, ...), kind=kLoop, calls=%fused_computation.275 | loop fusion | flops 7864320 | bytes 13766660 | tf_op jit(solution)/shard_map/mul | solution.py:84
  206.5 5.7 %collective-permute-start.30 = (f32[34,1,256]{2,1,0:T(1,128)S(1)}, f32[34,1,256]{2,1,0:T(1,128)S(1)}, u32[]{:S(2)}, u32[]{:S(2)}) collective-permute-start(f32[34,1,256]{2,1,0:T(1,128)S(1)} %get-tuple-element.39), channel_id=1, source_target_pairs={{0,1},{1,2},{2,3},{3,4},{4,5},{5,6},{6,7},{7,8},{8,9},{9,10},{10,1... | collective-permute-start | bytes 104456 | tf_op jit(solution)/shard_map/ppermute | solution.py:25
  214.2 4.9 %collective-permute-done.31 = f32[34,1,256]{2,1,0:T(1,128)S(1)} collective-permute-done((f32[34,1,256]{2,1,0:T(1,128)S(1)}, f32[34,1,256]{2,1,0:T(1,128)S(1)}, u32[]{:S(2)}, u32[]{:S(2)}) %collective-permute-start.31) | collective-permute-done | bytes 34848 | tf_op jit(solution)/shard_map/ppermute | solution.py:28
  220.0 3.5 %fusion.128 = (f32[32,32,256]{2,1,0:T(8,128)S(1)}, f32[32,32,256]{2,1,0:T(8,128)}) fusion(f32[32,32,256]{2,1,0:T(8,128)S(1)} %get-tuple-element.20, f32[32,32,256]{2,1,0:T(8,128)S(1)} %get-tuple-element.21, f32[32,32,256]{2,1,0:T(8,128)S(1)} %copy-done.7, f32[34,34,258]{2,1,0:T(8,128)S(1)} %select_maximum_fusion.8, f32[32,32,256]{2,1,0:T(8,128)S(1)} %copy-done.4, ...), kind=kLoop, calls=%fused_computation.307 | loop fusion | flops 8650752 | bytes 12718080 | tf_op jit(solution)/shard_map/add | solution.py:86
  223.5 3.3 %collective-permute-start.32 = (f32[1,32,256]{2,1,0:T(8,128)S(1)}, f32[1,32,256]{2,1,0:T(8,128)S(1)}, u32[]{:S(2)}, u32[]{:S(2)}) collective-permute-start(f32[1,32,256]{2,1,0:T(8,128)S(1)} %get-tuple-element.57), channel_id=1, source_target_pairs={{0,16},{16,32},{32,48},{48,64},{64,80},{80,96},{96,112},{1,17},{17... | collective-permute-start | bytes 98312 | tf_op jit(solution)/shard_map/ppermute | solution.py:25
  228.8 3.3 %collective-permute-done.33 = f32[1,32,256]{2,1,0:T(8,128)S(1)} collective-permute-done((f32[1,32,256]{2,1,0:T(8,128)S(1)}, f32[1,32,256]{2,1,0:T(8,128)S(1)}, u32[]{:S(2)}, u32[]{:S(2)}) %collective-permute-start.33) | collective-permute-done | bytes 32800 | tf_op jit(solution)/shard_map/ppermute | solution.py:28
  234.1 3.4 %collective-permute-start.35 = (f32[34,1,256]{2,1,0:T(1,128)S(1)}, f32[34,1,256]{2,1,0:T(1,128)S(1)}, u32[]{:S(2)}, u32[]{:S(2)}) collective-permute-start(f32[34,1,256]{2,1,0:T(1,128)S(1)} %get-tuple-element.38), channel_id=1, source_target_pairs={{1,0},{2,1},{3,2},{4,3},{5,4},{6,5},{7,6},{8,7},{9,8},{10,9},{11,1... | collective-permute-start | bytes 104456 | tf_op jit(solution)/shard_map/ppermute | solution.py:28
  238.7 24.4 %all-reduce.10 = (f32[]{:T(128)}, f32[]{:T(128)}) all-reduce(f32[]{:T(128)} %get-tuple-element.5, f32[]{:T(128)} %get-tuple-element.4), channel_id=1, replica_groups=mesh['gx'=8,'gy'=16] {'gy'}, use_global_device_ids=true, to_apply=%region_7.8 | all-reduce | flops 2 | bytes 16 | tf_op jit(solution)/shard_map/psum | solution.py:102
  263.1 18.4 %all-reduce.12 = (f32[]{:T(128)}, f32[]{:T(128)}) all-reduce(f32[]{:T(128)} %get-tuple-element.8, f32[]{:T(128)} %get-tuple-element.9), channel_id=1, replica_groups=mesh['gx'=8,'gy'=16] {'gx'}, use_global_device_ids=true, to_apply=%region_8.9 | all-reduce | flops 2 | bytes 16 | tf_op jit(solution)/shard_map/psum | solution.py:101
  288.5 7.4 %multiply_subtract_fusion = (f32[32,32,256]{2,1,0:T(8,128)}, f32[32,32,256]{2,1,0:T(8,128)S(1)}) fusion(f32[32,32,256]{2,1,0:T(8,128)} %copy-done.9, f32[]{:T(128)S(6)} %div.70, f32[]{:T(128)S(6)} %div.72, f32[32,32,256]{2,1,0:T(8,128)} %copy-done.12, f32[]{:T(128)S(6)} %div.66, f32[32,32,256]{2,1,0:T(8,128)} %copy-done.23, f32[32,32,256]{2,1,0:T(8,128)} %copy-done.18, ...), kind=kLoop, calls=%fused_computation.254 | loop fusion | flops 9961472 | bytes 15863820 | tf_op jit(solution)/shard_map/sub | solution.py:123
  303.5 5.7 %collective-permute-start.38 = (f32[34,1,256]{2,1,0:T(1,128)S(1)}, f32[34,1,256]{2,1,0:T(1,128)S(1)}, u32[]{:S(2)}, u32[]{:S(2)}) collective-permute-start(f32[34,1,256]{2,1,0:T(1,128)S(1)} %get-tuple-element.35), channel_id=1, source_target_pairs={{0,1},{1,2},{2,3},{3,4},{4,5},{5,6},{6,7},{7,8},{8,9},{9,10},{10,1... | collective-permute-start | bytes 104456 | tf_op jit(solution)/shard_map/ppermute | solution.py:25
  317.0 3.5 %fusion.5 = f32[32,32,256]{2,1,0:T(8,128)} fusion(f32[32,32,256]{2,1,0:T(8,128)S(1)} %copy-done.19, f32[32,32,256]{2,1,0:T(8,128)S(1)} %copy-done.8, f32[34,34,258]{2,1,0:T(8,128)S(1)} %select_maximum_fusion, f32[32,32,256]{2,1,0:T(8,128)S(1)} %copy-done.5, f32[32,32,256]{2,1,0:T(8,128)S(1)} %copy-done.2, f32[34,1,256]{2,1,0:T(1,128)S(1)} %collective-permute-done.39, ...), kind=kLoop, calls=%fused_computation.49 | loop fusion | flops 7864320 | bytes 12718088 | tf_op jit(solution)/shard_map/sub | solution.py:124
  (152 shorter events, 117.5 us)
Async XLA Ops:
  1.4 5.7 %collective-permute-start = (s32[1,32,256]{2,1,0:T(8,128)S(1)}, s32[1,32,256]{2,1,0:T(8,128)S(1)}, u32[]{:S(2)}, u32[]{:S(2)}) collective-permute-start(s32[1,32,256]{2,1,0:T(8,128)S(1)} %get-tuple-element.74), channel_id=1, source_target_pairs={{0,16},{16,32},{32,48},{48,64},{64,80},{80,96},{96,112},{1,17},{17... | collective-permute-start | bytes 98312 | tf_op jit(solution)/shard_map/ppermute | solution.py:25
  5.2 5.2 %collective-permute-start.1 = (s32[1,32,256]{2,1,0:T(8,128)S(1)}, s32[1,32,256]{2,1,0:T(8,128)S(1)}, u32[]{:S(2)}, u32[]{:S(2)}) collective-permute-start(s32[1,32,256]{2,1,0:T(8,128)S(1)} %get-tuple-element.73), channel_id=1, source_target_pairs={{16,0},{32,16},{48,32},{64,48},{80,64},{96,80},{112,96},{17,1},{33... | collective-permute-start | bytes 98312 | tf_op jit(solution)/shard_map/ppermute | solution.py:28
  10.5 6.0 %collective-permute-start.2 = (s32[34,1,256]{2,1,0:T(1,128)S(1)}, s32[34,1,256]{2,1,0:T(1,128)S(1)}, u32[]{:S(2)}, u32[]{:S(2)}) collective-permute-start(s32[34,1,256]{2,1,0:T(1,128)S(1)} %get-tuple-element.53), channel_id=1, source_target_pairs={{0,1},{1,2},{2,3},{3,4},{4,5},{5,6},{6,7},{7,8},{8,9},{9,10},{10,1... | collective-permute-start | bytes 104456 | tf_op jit(solution)/shard_map/ppermute | solution.py:25
  13.9 6.8 %collective-permute-start.3 = (s32[34,1,256]{2,1,0:T(1,128)S(1)}, s32[34,1,256]{2,1,0:T(1,128)S(1)}, u32[]{:S(2)}, u32[]{:S(2)}) collective-permute-start(s32[34,1,256]{2,1,0:T(1,128)S(1)} %get-tuple-element.54), channel_id=1, source_target_pairs={{1,0},{2,1},{3,2},{4,3},{5,4},{6,5},{7,6},{8,7},{9,8},{10,9},{11,1... | collective-permute-start | bytes 104456 | tf_op jit(solution)/shard_map/ppermute | solution.py:28
  26.5 5.3 %collective-permute-start.4 = (f32[1,32,256]{2,1,0:T(8,128)S(1)}, f32[1,32,256]{2,1,0:T(8,128)S(1)}, u32[]{:S(2)}, u32[]{:S(2)}) collective-permute-start(f32[1,32,256]{2,1,0:T(8,128)S(1)} %get-tuple-element.71), channel_id=1, source_target_pairs={{0,16},{16,32},{32,48},{48,64},{64,80},{80,96},{96,112},{1,17},{17... | collective-permute-start | bytes 98312 | tf_op jit(solution)/shard_map/ppermute | solution.py:25
  29.9 5.2 %collective-permute-start.5 = (f32[1,32,256]{2,1,0:T(8,128)S(1)}, f32[1,32,256]{2,1,0:T(8,128)S(1)}, u32[]{:S(2)}, u32[]{:S(2)}) collective-permute-start(f32[1,32,256]{2,1,0:T(8,128)S(1)} %get-tuple-element.72), channel_id=1, source_target_pairs={{16,0},{32,16},{48,32},{64,48},{80,64},{96,80},{112,96},{17,1},{33... | collective-permute-start | bytes 98312 | tf_op jit(solution)/shard_map/ppermute | solution.py:28
  35.2 5.3 %collective-permute-start.6 = (f32[34,1,256]{2,1,0:T(1,128)S(1)}, f32[34,1,256]{2,1,0:T(1,128)S(1)}, u32[]{:S(2)}, u32[]{:S(2)}) collective-permute-start(f32[34,1,256]{2,1,0:T(1,128)S(1)} %get-tuple-element.51), channel_id=1, source_target_pairs={{0,1},{1,2},{2,3},{3,4},{4,5},{5,6},{6,7},{7,8},{8,9},{9,10},{10,1... | collective-permute-start | bytes 104456 | tf_op jit(solution)/shard_map/ppermute | solution.py:25
  37.1 6.8 %collective-permute-start.7 = (f32[34,1,256]{2,1,0:T(1,128)S(1)}, f32[34,1,256]{2,1,0:T(1,128)S(1)}, u32[]{:S(2)}, u32[]{:S(2)}) collective-permute-start(f32[34,1,256]{2,1,0:T(1,128)S(1)} %get-tuple-element.52), channel_id=1, source_target_pairs={{1,0},{2,1},{3,2},{4,3},{5,4},{6,5},{7,6},{8,7},{9,8},{10,9},{11,1... | collective-permute-start | bytes 104456 | tf_op jit(solution)/shard_map/ppermute | solution.py:28
  50.6 5.2 %collective-permute-start.9 = (f32[1,32,256]{2,1,0:T(8,128)S(1)}, f32[1,32,256]{2,1,0:T(8,128)S(1)}, u32[]{:S(2)}, u32[]{:S(2)}) collective-permute-start(f32[1,32,256]{2,1,0:T(8,128)S(1)} %get-tuple-element.70), channel_id=1, source_target_pairs={{16,0},{32,16},{48,32},{64,48},{80,64},{96,80},{112,96},{17,1},{33... | collective-permute-start | bytes 98312 | tf_op jit(solution)/shard_map/ppermute | solution.py:28
  55.9 5.3 %collective-permute-start.10 = (f32[34,1,256]{2,1,0:T(1,128)S(1)}, f32[34,1,256]{2,1,0:T(1,128)S(1)}, u32[]{:S(2)}, u32[]{:S(2)}) collective-permute-start(f32[34,1,256]{2,1,0:T(1,128)S(1)} %get-tuple-element.49), channel_id=1, source_target_pairs={{0,1},{1,2},{2,3},{3,4},{4,5},{5,6},{6,7},{7,8},{8,9},{9,10},{10,1... | collective-permute-start | bytes 104456 | tf_op jit(solution)/shard_map/ppermute | solution.py:25
  57.8 6.8 %collective-permute-start.11 = (f32[34,1,256]{2,1,0:T(1,128)S(1)}, f32[34,1,256]{2,1,0:T(1,128)S(1)}, u32[]{:S(2)}, u32[]{:S(2)}) collective-permute-start(f32[34,1,256]{2,1,0:T(1,128)S(1)} %get-tuple-element.50), channel_id=1, source_target_pairs={{1,0},{2,1},{3,2},{4,3},{5,4},{6,5},{7,6},{8,7},{9,8},{10,9},{11,1... | collective-permute-start | bytes 104456 | tf_op jit(solution)/shard_map/ppermute | solution.py:28
  71.4 5.2 %collective-permute-start.13 = (f32[1,32,256]{2,1,0:T(8,128)S(1)}, f32[1,32,256]{2,1,0:T(8,128)S(1)}, u32[]{:S(2)}, u32[]{:S(2)}) collective-permute-start(f32[1,32,256]{2,1,0:T(8,128)S(1)} %get-tuple-element.68), channel_id=1, source_target_pairs={{16,0},{32,16},{48,32},{64,48},{80,64},{96,80},{112,96},{17,1},{33... | collective-permute-start | bytes 98312 | tf_op jit(solution)/shard_map/ppermute | solution.py:28
  76.7 5.3 %collective-permute-start.14 = (f32[34,1,256]{2,1,0:T(1,128)S(1)}, f32[34,1,256]{2,1,0:T(1,128)S(1)}, u32[]{:S(2)}, u32[]{:S(2)}) collective-permute-start(f32[34,1,256]{2,1,0:T(1,128)S(1)} %get-tuple-element.47), channel_id=1, source_target_pairs={{0,1},{1,2},{2,3},{3,4},{4,5},{5,6},{6,7},{7,8},{8,9},{9,10},{10,1... | collective-permute-start | bytes 104456 | tf_op jit(solution)/shard_map/ppermute | solution.py:25
  78.6 6.8 %collective-permute-start.15 = (f32[34,1,256]{2,1,0:T(1,128)S(1)}, f32[34,1,256]{2,1,0:T(1,128)S(1)}, u32[]{:S(2)}, u32[]{:S(2)}) collective-permute-start(f32[34,1,256]{2,1,0:T(1,128)S(1)} %get-tuple-element.48), channel_id=1, source_target_pairs={{1,0},{2,1},{3,2},{4,3},{5,4},{6,5},{7,6},{8,7},{9,8},{10,9},{11,1... | collective-permute-start | bytes 104456 | tf_op jit(solution)/shard_map/ppermute | solution.py:28
  93.5 5.2 %collective-permute-start.17 = (f32[1,32,256]{2,1,0:T(8,128)S(1)}, f32[1,32,256]{2,1,0:T(8,128)S(1)}, u32[]{:S(2)}, u32[]{:S(2)}) collective-permute-start(f32[1,32,256]{2,1,0:T(8,128)S(1)} %get-tuple-element.66), channel_id=1, source_target_pairs={{16,0},{32,16},{48,32},{64,48},{80,64},{96,80},{112,96},{17,1},{33... | collective-permute-start | bytes 98312 | tf_op jit(solution)/shard_map/ppermute | solution.py:28
  98.8 5.5 %collective-permute-start.18 = (f32[34,1,256]{2,1,0:T(1,128)S(1)}, f32[34,1,256]{2,1,0:T(1,128)S(1)}, u32[]{:S(2)}, u32[]{:S(2)}) collective-permute-start(f32[34,1,256]{2,1,0:T(1,128)S(1)} %get-tuple-element.45), channel_id=1, source_target_pairs={{0,1},{1,2},{2,3},{3,4},{4,5},{5,6},{6,7},{7,8},{8,9},{9,10},{10,1... | collective-permute-start | bytes 104456 | tf_op jit(solution)/shard_map/ppermute | solution.py:25
  100.7 6.8 %collective-permute-start.19 = (f32[34,1,256]{2,1,0:T(1,128)S(1)}, f32[34,1,256]{2,1,0:T(1,128)S(1)}, u32[]{:S(2)}, u32[]{:S(2)}) collective-permute-start(f32[34,1,256]{2,1,0:T(1,128)S(1)} %get-tuple-element.46), channel_id=1, source_target_pairs={{1,0},{2,1},{3,2},{4,3},{5,4},{6,5},{7,6},{8,7},{9,8},{10,9},{11,1... | collective-permute-start | bytes 104456 | tf_op jit(solution)/shard_map/ppermute | solution.py:28
  114.3 5.2 %collective-permute-start.21 = (f32[1,32,256]{2,1,0:T(8,128)S(1)}, f32[1,32,256]{2,1,0:T(8,128)S(1)}, u32[]{:S(2)}, u32[]{:S(2)}) collective-permute-start(f32[1,32,256]{2,1,0:T(8,128)S(1)} %get-tuple-element.64), channel_id=1, source_target_pairs={{16,0},{32,16},{48,32},{64,48},{80,64},{96,80},{112,96},{17,1},{33... | collective-permute-start | bytes 98312 | tf_op jit(solution)/shard_map/ppermute | solution.py:28
  119.5 5.3 %collective-permute-start.22 = (f32[34,1,256]{2,1,0:T(1,128)S(1)}, f32[34,1,256]{2,1,0:T(1,128)S(1)}, u32[]{:S(2)}, u32[]{:S(2)}) collective-permute-start(f32[34,1,256]{2,1,0:T(1,128)S(1)} %get-tuple-element.43), channel_id=1, source_target_pairs={{0,1},{1,2},{2,3},{3,4},{4,5},{5,6},{6,7},{7,8},{8,9},{9,10},{10,1... | collective-permute-start | bytes 104456 | tf_op jit(solution)/shard_map/ppermute | solution.py:25
  121.5 6.8 %collective-permute-start.23 = (f32[34,1,256]{2,1,0:T(1,128)S(1)}, f32[34,1,256]{2,1,0:T(1,128)S(1)}, u32[]{:S(2)}, u32[]{:S(2)}) collective-permute-start(f32[34,1,256]{2,1,0:T(1,128)S(1)} %get-tuple-element.44), channel_id=1, source_target_pairs={{1,0},{2,1},{3,2},{4,3},{5,4},{6,5},{7,6},{8,7},{9,8},{10,9},{11,1... | collective-permute-start | bytes 104456 | tf_op jit(solution)/shard_map/ppermute | solution.py:28
  135.1 5.2 %collective-permute-start.25 = (f32[1,32,256]{2,1,0:T(8,128)S(1)}, f32[1,32,256]{2,1,0:T(8,128)S(1)}, u32[]{:S(2)}, u32[]{:S(2)}) collective-permute-start(f32[1,32,256]{2,1,0:T(8,128)S(1)} %get-tuple-element.62), channel_id=1, source_target_pairs={{16,0},{32,16},{48,32},{64,48},{80,64},{96,80},{112,96},{17,1},{33... | collective-permute-start | bytes 98312 | tf_op jit(solution)/shard_map/ppermute | solution.py:28
  140.4 49.9 %collective-permute-start.26 = (f32[34,1,256]{2,1,0:T(1,128)S(1)}, f32[34,1,256]{2,1,0:T(1,128)S(1)}, u32[]{:S(2)}, u32[]{:S(2)}) collective-permute-start(f32[34,1,256]{2,1,0:T(1,128)S(1)} %get-tuple-element.41), channel_id=1, source_target_pairs={{0,1},{1,2},{2,3},{3,4},{4,5},{5,6},{6,7},{7,8},{8,9},{9,10},{10,1... | collective-permute-start | bytes 104456 | tf_op jit(solution)/shard_map/ppermute | solution.py:25
  142.3 48.0 %collective-permute-start.27 = (f32[34,1,256]{2,1,0:T(1,128)S(1)}, f32[34,1,256]{2,1,0:T(1,128)S(1)}, u32[]{:S(2)}, u32[]{:S(2)}) collective-permute-start(f32[34,1,256]{2,1,0:T(1,128)S(1)} %get-tuple-element.42), channel_id=1, source_target_pairs={{1,0},{2,1},{3,2},{4,3},{5,4},{6,5},{7,6},{8,7},{9,8},{10,9},{11,1... | collective-permute-start | bytes 104456 | tf_op jit(solution)/shard_map/ppermute | solution.py:28
  201.2 5.2 %collective-permute-start.29 = (f32[1,32,256]{2,1,0:T(8,128)S(1)}, f32[1,32,256]{2,1,0:T(8,128)S(1)}, u32[]{:S(2)}, u32[]{:S(2)}) collective-permute-start(f32[1,32,256]{2,1,0:T(8,128)S(1)} %get-tuple-element.60), channel_id=1, source_target_pairs={{16,0},{32,16},{48,32},{64,48},{80,64},{96,80},{112,96},{17,1},{33... | collective-permute-start | bytes 98312 | tf_op jit(solution)/shard_map/ppermute | solution.py:28
  206.5 7.7 %collective-permute-start.30 = (f32[34,1,256]{2,1,0:T(1,128)S(1)}, f32[34,1,256]{2,1,0:T(1,128)S(1)}, u32[]{:S(2)}, u32[]{:S(2)}) collective-permute-start(f32[34,1,256]{2,1,0:T(1,128)S(1)} %get-tuple-element.39), channel_id=1, source_target_pairs={{0,1},{1,2},{2,3},{3,4},{4,5},{5,6},{6,7},{7,8},{8,9},{9,10},{10,1... | collective-permute-start | bytes 104456 | tf_op jit(solution)/shard_map/ppermute | solution.py:25
  212.2 6.8 %collective-permute-start.31 = (f32[34,1,256]{2,1,0:T(1,128)S(1)}, f32[34,1,256]{2,1,0:T(1,128)S(1)}, u32[]{:S(2)}, u32[]{:S(2)}) collective-permute-start(f32[34,1,256]{2,1,0:T(1,128)S(1)} %get-tuple-element.40), channel_id=1, source_target_pairs={{1,0},{2,1},{3,2},{4,3},{5,4},{6,5},{7,6},{8,7},{9,8},{10,9},{11,1... | collective-permute-start | bytes 104456 | tf_op jit(solution)/shard_map/ppermute | solution.py:28
  223.5 5.3 %collective-permute-start.32 = (f32[1,32,256]{2,1,0:T(8,128)S(1)}, f32[1,32,256]{2,1,0:T(8,128)S(1)}, u32[]{:S(2)}, u32[]{:S(2)}) collective-permute-start(f32[1,32,256]{2,1,0:T(8,128)S(1)} %get-tuple-element.57), channel_id=1, source_target_pairs={{0,16},{16,32},{32,48},{48,64},{64,80},{80,96},{96,112},{1,17},{17... | collective-permute-start | bytes 98312 | tf_op jit(solution)/shard_map/ppermute | solution.py:25
  226.9 5.2 %collective-permute-start.33 = (f32[1,32,256]{2,1,0:T(8,128)S(1)}, f32[1,32,256]{2,1,0:T(8,128)S(1)}, u32[]{:S(2)}, u32[]{:S(2)}) collective-permute-start(f32[1,32,256]{2,1,0:T(8,128)S(1)} %get-tuple-element.58), channel_id=1, source_target_pairs={{16,0},{32,16},{48,32},{64,48},{80,64},{96,80},{112,96},{17,1},{33... | collective-permute-start | bytes 98312 | tf_op jit(solution)/shard_map/ppermute | solution.py:28
  232.2 54.0 %collective-permute-start.34 = (f32[34,1,256]{2,1,0:T(1,128)S(1)}, f32[34,1,256]{2,1,0:T(1,128)S(1)}, u32[]{:S(2)}, u32[]{:S(2)}) collective-permute-start(f32[34,1,256]{2,1,0:T(1,128)S(1)} %get-tuple-element.37), channel_id=1, source_target_pairs={{0,1},{1,2},{2,3},{3,4},{4,5},{5,6},{6,7},{7,8},{8,9},{9,10},{10,1... | collective-permute-start | bytes 104456 | tf_op jit(solution)/shard_map/ppermute | solution.py:25
  234.1 52.1 %collective-permute-start.35 = (f32[34,1,256]{2,1,0:T(1,128)S(1)}, f32[34,1,256]{2,1,0:T(1,128)S(1)}, u32[]{:S(2)}, u32[]{:S(2)}) collective-permute-start(f32[34,1,256]{2,1,0:T(1,128)S(1)} %get-tuple-element.38), channel_id=1, source_target_pairs={{1,0},{2,1},{3,2},{4,3},{5,4},{6,5},{7,6},{8,7},{9,8},{10,9},{11,1... | collective-permute-start | bytes 104456 | tf_op jit(solution)/shard_map/ppermute | solution.py:28
  303.5 9.7 %collective-permute-start.38 = (f32[34,1,256]{2,1,0:T(1,128)S(1)}, f32[34,1,256]{2,1,0:T(1,128)S(1)}, u32[]{:S(2)}, u32[]{:S(2)}) collective-permute-start(f32[34,1,256]{2,1,0:T(1,128)S(1)} %get-tuple-element.35), channel_id=1, source_target_pairs={{0,1},{1,2},{2,3},{3,4},{4,5},{5,6},{6,7},{7,8},{8,9},{9,10},{10,1... | collective-permute-start | bytes 104456 | tf_op jit(solution)/shard_map/ppermute | solution.py:25
  309.3 6.8 %collective-permute-start.39 = (f32[34,1,256]{2,1,0:T(1,128)S(1)}, f32[34,1,256]{2,1,0:T(1,128)S(1)}, u32[]{:S(2)}, u32[]{:S(2)}) collective-permute-start(f32[34,1,256]{2,1,0:T(1,128)S(1)} %get-tuple-element.36), channel_id=1, source_target_pairs={{1,0},{2,1},{3,2},{4,3},{5,4},{6,5},{7,6},{8,7},{9,8},{10,9},{11,1... | collective-permute-start | bytes 104456 | tf_op jit(solution)/shard_map/ppermute | solution.py:28
  (34 other events, 686.5 us)
